TPU v7x, 32 devices: a whole 2x2x4 slice. The times are simulated.
32 devices in a mesh: dp: 4 (over z), fsdp: 8 (over y, x, core).
Axes of the slice: x: 2, y: 2, z: 4, core: 2. Of those that a mesh axis runs over, the one named last changes fastest.
Arguments:
- tokens: bfloat16 [4096, 2048], P(('dp', 'fsdp')), may hold values from -6 to 6
- ln_gain: float32 [2048], replicated, may hold values from 0.5 to 1.5
- ln_shift: float32 [2048], replicated, may hold values from -3 to 3
- w_qkv: bfloat16 [2048, 6144], P(('dp', 'fsdp')), may hold values from -0.125 to 0.125
- b_qkv: float32 [6144], replicated, may hold values from -3 to 3
- w_out: bfloat16 [2048, 2048], P(('dp', 'fsdp')), may hold values from -0.5 to 0.5
- w_gate: bfloat16 [2048, 5632], P(('dp', 'fsdp')), may hold values from -0.125 to 0.125
- w_up: bfloat16 [2048, 5632], P(('dp', 'fsdp')), may hold values from -0.125 to 0.125
- w_down: bfloat16 [5632, 2048], P(('dp', 'fsdp')), may hold values from -0.078125 to 0.078125
- grad_out: bfloat16 [4096, 2048], P(('dp', 'fsdp')), may hold values from -6 to 6
- seq_lengths: int32 [32, 4], P(('dp', 'fsdp')), may hold values from 0 to 128, as said below
Outputs:
- output: bfloat16 [4096, 2048], P(('dp', 'fsdp'))
- grad_tokens: bfloat16 [4096, 2048], P(('dp', 'fsdp'))
- grad_w_qkv: float32 [2048, 6144], P(('dp', 'fsdp'))
- grad_w_out: float32 [2048, 2048], P(('dp', 'fsdp'))
- grad_w_gate: float32 [2048, 5632], P(('dp', 'fsdp'))
- grad_w_up: float32 [2048, 5632], P(('dp', 'fsdp'))
- grad_w_down: float32 [5632, 2048], P(('dp', 'fsdp'))
- grad_gain: float32 [2048], P(('dp', 'fsdp'))
- grad_shift: float32 [2048], P(('dp', 'fsdp'))
- grad_bias: float32 [6144], P(('dp', 'fsdp'))
Inputs may be any that keep to these rules, and one draw needn't show every extreme that they name: `seq_lengths`: each device's row of lengths sums to at most 128; some device holds a single sequence of exactly 128 tokens, and some slots are empty (length 0).
All inputs are finite; a program needn't handle non-finite values.
Results may differ from a plain program's by a relative error of at most 0.012.
Values may be sent and summed in bfloat16 or wider, within the bound.
No kernel may reach another device: no remote copies, remote signals or barrier semaphores. Data moves between devices by JAX's collectives and lax.ppermute only.
A program may use at most 256 MiB of HBM per device.

v0:
```python
import math
import jax
import jax.numpy as jnp
from jax import lax
from jax.sharding import PartitionSpec as P

HD = 64
ROT = 16
EPS = 1e-05
NEG = -1e30
CONTRACT_ROWS = (((0,), (0,)), ((), ()))
CONTRACT_COLS = (((1,), (1,)), ((), ()))


def block_terms(lengths_row, rows_tok):
    ends = jnp.cumsum(lengths_row)
    place = jnp.arange(rows_tok, dtype=jnp.int32)
    segment = jnp.sum((place[:, None] >= ends[None, :]).astype(jnp.int32), axis=1)
    starts = jnp.concatenate([ends - lengths_row, ends[-1:]])
    labels = jnp.arange(starts.shape[0], dtype=jnp.int32)
    begin = jnp.sum(jnp.where(segment[:, None] == labels[None, :], starts[None, :], 0), axis=1)
    position = (place - begin).astype(jnp.float32)
    valid = segment < lengths_row.shape[0]
    label_tok = jnp.where(valid, segment, lengths_row.shape[0] + place)
    allowed = (label_tok[:, None] == label_tok[None, :]) & (place[None, :] <= place[:, None])
    return (position, valid, allowed)


def angles(position):
    half = ROT // 2
    freq = jnp.exp(jnp.arange(half, dtype=jnp.float32) * (-2.0 * math.log(10000.0) / ROT))
    turn = position[:, None] * freq[None, :]
    return (jnp.cos(turn), jnp.sin(turn))


def rotate(heads_in, cosine, sine):
    half = ROT // 2
    first = heads_in[..., :half]
    second = heads_in[..., half:ROT]
    cos_b = cosine[:, None, :]
    sin_b = sine[:, None, :]
    return jnp.concatenate(
        [first * cos_b - second * sin_b, second * cos_b + first * sin_b, heads_in[..., ROT:]],
        axis=-1,
    )


def alternate(first, second, shards):
    rows_tok = first.shape[0]
    joined = jnp.concatenate(
        [first.reshape(rows_tok, shards, -1), second.reshape(rows_tok, shards, -1)], axis=2
    )
    return joined.reshape(rows_tok, -1)


def separate(joined, shards, split_at):
    rows_tok = joined.shape[0]
    blocks = joined.reshape(rows_tok, shards, -1)
    return (
        blocks[:, :, :split_at].reshape(rows_tok, -1),
        blocks[:, :, split_at:].reshape(rows_tok, -1),
    )


def on_device(
    tokens, ln_gain, ln_shift, w_qkv, b_qkv, w_out, w_gate, w_up, w_down, grad_out, seq_lengths
):
    shards = lax.axis_size(("dp", "fsdp"))
    rows_tok, width = tokens.shape
    heads = width // HD
    inner = w_gate.shape[1]
    own_rows = w_qkv.shape[0]
    position, valid, allowed = block_terms(seq_lengths[0], rows_tok)
    cosine, sine = angles(position)
    keep_row = valid.astype(jnp.float32)[:, None]
    widened = tokens.astype(jnp.float32)
    centered = widened - jnp.mean(widened, axis=1, keepdims=True)
    inv_std = lax.rsqrt(jnp.mean(centered * centered, axis=1, keepdims=True) + EPS)
    scaled = centered * inv_std
    normed = (scaled * ln_gain + ln_shift).astype(jnp.bfloat16)
    mixer = jnp.concatenate([w_out, w_down], axis=0)
    pieces = (
        lax.all_gather(w_qkv, ("dp", "fsdp"), axis=0, tiled=True),
        lax.all_gather(w_gate, ("dp", "fsdp"), axis=0, tiled=True),
        lax.all_gather(w_up, ("dp", "fsdp"), axis=0, tiled=True),
    )
    columns = normed
    proj_qkv, proj_gate, proj_up = tuple(
        (jnp.dot(columns, piece, preferred_element_type=jnp.float32) for piece in pieces)
    )
    split_qkv = (proj_qkv + b_qkv).reshape(rows_tok, 3, heads, HD)
    query = rotate(split_qkv[:, 0], cosine, sine).astype(jnp.bfloat16)
    keys = rotate(split_qkv[:, 1], cosine, sine).astype(jnp.bfloat16)
    values = split_qkv[:, 2].astype(jnp.bfloat16)
    scores = jnp.einsum("qhd,khd->hqk", query, keys, preferred_element_type=jnp.float32) * 0.125
    scores = jnp.where(allowed[None], scores, NEG)
    peak = jnp.max(scores, axis=2, keepdims=True)
    lifted = jnp.exp(scores - peak)
    row_total = jnp.sum(lifted, axis=2, keepdims=True)
    probs = lifted / row_total
    log_total = peak + jnp.log(row_total)
    attended = jnp.einsum(
        "hqk,khd->qhd", probs.astype(jnp.bfloat16), values, preferred_element_type=jnp.float32
    )
    attended = attended.reshape(rows_tok, width).astype(jnp.bfloat16)
    sigma = jax.nn.sigmoid(proj_gate)
    activ = proj_gate * sigma
    hidden = (activ * proj_up).astype(jnp.bfloat16)
    joined = alternate(attended, hidden, shards)
    columns = joined
    branch_sum = jnp.dot(
        columns,
        lax.all_gather(mixer, ("dp", "fsdp"), axis=0, tiled=True),
        preferred_element_type=jnp.float32,
    )
    output = (widened + keep_row * branch_sum).astype(jnp.bfloat16)
    masked = (grad_out.astype(jnp.float32) * keep_row).astype(jnp.bfloat16)
    back_mix = lax.dot_general(
        masked,
        lax.all_gather(mixer, ("dp", "fsdp"), axis=0, tiled=True),
        CONTRACT_COLS,
        preferred_element_type=jnp.float32,
    )
    grad_att, grad_hid = separate(back_mix, shards, own_rows)
    grad_mixed = grad_att.astype(jnp.bfloat16).reshape(rows_tok, heads, HD)
    redo = jnp.einsum("qhd,khd->hqk", query, keys, preferred_element_type=jnp.float32) * 0.125
    redo = jnp.where(allowed[None], redo, NEG)
    probs_again = jnp.exp(redo - log_total)
    grad_probs = jnp.einsum("qhd,khd->hqk", grad_mixed, values, preferred_element_type=jnp.float32)
    inner_sum = jnp.sum(probs_again * grad_probs, axis=2, keepdims=True)
    grad_scores = (probs_again * (grad_probs - inner_sum)).astype(jnp.bfloat16)
    grad_query = (
        jnp.einsum("hqk,khd->qhd", grad_scores, keys, preferred_element_type=jnp.float32) * 0.125
    )
    grad_keys = (
        jnp.einsum("hqk,qhd->khd", grad_scores, query, preferred_element_type=jnp.float32) * 0.125
    )
    grad_values = jnp.einsum(
        "hqk,qhd->khd",
        probs_again.astype(jnp.bfloat16),
        grad_mixed,
        preferred_element_type=jnp.float32,
    )
    grad_proj = jnp.stack(
        [rotate(grad_query, cosine, -sine), rotate(grad_keys, cosine, -sine), grad_values], axis=1
    )
    grad_proj = grad_proj.reshape(rows_tok, 3 * width).astype(jnp.bfloat16)
    slope = sigma * (1.0 + proj_gate * (1.0 - sigma))
    grad_gate = (grad_hid * proj_up * slope).astype(jnp.bfloat16)
    grad_up = (grad_hid * activ).astype(jnp.bfloat16)
    pieces = lax.all_gather((w_qkv, w_gate, w_up), ("dp", "fsdp"), axis=0, tiled=True)
    first = lax.dot_general(grad_proj, pieces[0], CONTRACT_COLS, preferred_element_type=jnp.float32)
    second = lax.dot_general(
        grad_gate, pieces[1], CONTRACT_COLS, preferred_element_type=jnp.float32
    )
    third = lax.dot_general(grad_up, pieces[2], CONTRACT_COLS, preferred_element_type=jnp.float32)
    grad_norm = first + second + third
    gain_part = jnp.sum(grad_norm * scaled, axis=0)
    shift_part = jnp.sum(grad_norm, axis=0)
    bias_part = jnp.sum(grad_proj.astype(jnp.float32), axis=0).reshape(width, 3)
    lifted_grad = grad_norm * ln_gain
    grad_in = inv_std * (
        lifted_grad
        - jnp.mean(lifted_grad, axis=1, keepdims=True)
        - scaled * jnp.mean(lifted_grad * scaled, axis=1, keepdims=True)
    )
    grad_tokens = (grad_out.astype(jnp.float32) + grad_in).astype(jnp.bfloat16)
    stats = jnp.concatenate(
        [gain_part[:, None], shift_part[:, None], bias_part, jnp.zeros((width, 123), jnp.float32)],
        axis=1,
    )
    outer = lax.axis_size("fsdp")
    group_rows = own_rows * outer
    normed_cols, joined_cols = (
        lax.all_to_all(normed, "dp", split_axis=1, concat_axis=0, tiled=True),
        lax.all_to_all(joined, "dp", split_axis=1, concat_axis=0, tiled=True),
    )
    stat_parts = lax.all_to_all(jnp.transpose(stats), "dp", split_axis=1, concat_axis=0, tiled=True)
    stat_sum = jnp.transpose(jnp.sum(stat_parts.reshape(-1, stats.shape[1], group_rows), axis=0))
    pieces = (
        lax.all_gather(grad_proj, "dp", axis=0, tiled=True),
        lax.all_gather(grad_gate, "dp", axis=0, tiled=True),
        lax.all_gather(grad_up, "dp", axis=0, tiled=True),
        lax.all_gather(masked, "dp", axis=0, tiled=True),
    )
    blocks = [
        lax.dot_general(normed_cols, piece, CONTRACT_ROWS, preferred_element_type=jnp.float32)
        for piece in pieces[:3]
    ]
    mixed_part = lax.dot_general(
        joined_cols, pieces[3], CONTRACT_ROWS, preferred_element_type=jnp.float32
    )
    input_part = jnp.concatenate(blocks, axis=1)
    input_part = jnp.concatenate([input_part, stat_sum], axis=1)
    input_sum, mixer_sum = (
        lax.psum_scatter(
            input_part.astype(jnp.bfloat16), "fsdp", scatter_dimension=0, tiled=True
        ).astype(jnp.float32),
        lax.psum_scatter(
            mixed_part.astype(jnp.bfloat16), "fsdp", scatter_dimension=0, tiled=True
        ).astype(jnp.float32),
    )
    qkv_cols = 3 * width
    grad_w_qkv = input_sum[:, :qkv_cols]
    grad_w_gate = input_sum[:, qkv_cols : qkv_cols + inner]
    grad_w_up = input_sum[:, qkv_cols + inner : qkv_cols + 2 * inner]
    tail_cols = input_sum[:, qkv_cols + 2 * inner :]
    grad_gain = tail_cols[:, 0]
    grad_shift = tail_cols[:, 1]
    grad_bias = tail_cols[:, 2:5].reshape(-1)
    grad_w_out = mixer_sum[:own_rows]
    grad_w_down = mixer_sum[own_rows:]
    return (
        output,
        grad_tokens,
        grad_w_qkv,
        grad_w_out,
        grad_w_gate,
        grad_w_up,
        grad_w_down,
        grad_gain,
        grad_shift,
        grad_bias,
    )


def solution(mesh):
    placed = (
        P(("dp", "fsdp"), None),
        P(),
        P(),
        P(("dp", "fsdp"), None),
        P(),
        P(("dp", "fsdp"), None),
        P(("dp", "fsdp"), None),
        P(("dp", "fsdp"), None),
        P(("dp", "fsdp"), None),
        P(("dp", "fsdp"), None),
        P(("dp", "fsdp"), None),
    )
    return jax.shard_map(
        on_device,
        mesh=mesh,
        in_specs=placed,
        out_specs=(
            P(("dp", "fsdp"), None),
            P(("dp", "fsdp"), None),
            P(("dp", "fsdp"), None),
            P(("dp", "fsdp"), None),
            P(("dp", "fsdp"), None),
            P(("dp", "fsdp"), None),
            P(("dp", "fsdp"), None),
            P(("dp", "fsdp")),
            P(("dp", "fsdp")),
            P(("dp", "fsdp")),
        ),
        check_vma=False,
    )
```

profile of v0, /device:TPU:0, one launch (start us, length us, event | category | flops | bytes accessed | tf_op | source)
XLA Modules:
  0.0 1287.0 jit_solution(11946301939778246751)
XLA Ops:
  7.2 0.7 all-gather.13.cloned.1.call-update
  8.0 2.3 pad_maximum_fusion.2
  10.3 0.7 all-gather.11.cloned.1.call-update
  11.1 0.5 all-gather.9.cloned.1.call-update
  11.9 0.9 fusion.21
  13.9 144.3 %all-gather.13.cloned.1.call-done = bf16[2048,5632]{1,0:T(8,128)(2,1)} async-done(((bf16[64,5632]{1,0:T(8,128)(2,1)}), bf16[2048,5632]{1,0:T(8,128)(2,1)}) %all-gather.13.cloned.1.call-update) | async-done | bytes 23068688 | tf_op jit(solution)/shard_map/all_gather | solution.py:85
  158.2 12.3 fusion.36
  170.5 174.2 %all-gather.15.cloned.1.call-done = bf16[7680,2048]{1,0:T(8,128)(2,1)} async-done(((bf16[240,2048]{1,0:T(8,128)(2,1)}), bf16[7680,2048]{1,0:T(8,128)(2,1)}) %all-gather.15.cloned.1.call-update) | async-done | bytes 31457296 | tf_op jit(solution)/shard_map/all_gather | solution.py:113
  344.7 14.4 %fusion.37 = f32[128,7680]{0,1:T(8,128)S(1)} fusion(bf16[128,2048]{1,0:T(8,128)(2,1)S(1)} %copy-done.8, bf16[7680,2048]{1,0:T(8,128)(2,1)} %all-gather.15.cloned.1.call-done), kind=kOutput, calls=%fused_computation.107 | convolution fusion | flops 4026531840 | bytes 35913728 | tf_op jit(solution)/shard_map/dot_general | solution.py:118
  359.1 2.0 slice.132
  361.1 0.8 copy-done.3
  361.9 3.4 copy.50
  365.3 125.1 %all-gather.11.cloned.1.call-done = bf16[2048,5632]{1,0:T(8,128)(2,1)} async-done(((bf16[64,5632]{1,0:T(8,128)(2,1)}), bf16[2048,5632]{1,0:T(8,128)(2,1)}) %all-gather.11.cloned.1.call-update) | async-done | bytes 23068688 | tf_op jit(solution)/shard_map/all_gather | solution.py:84
  490.4 15.8 %multiply_convert_fusion = (bf16[128,5632]{1,0:T(8,128)(2,1)}, bf16[128,5632]{1,0:T(8,128)(2,1)}, bf16[128,5632]{1,0:T(8,128)(2,1)}) fusion(f32[128,5632]{1,0:T(8,128)} %copy.50, f32[128,5632]{1,0:T(8,128)} %fusion.36, bf16[128,2048]{1,0:T(8,128)(2,1)S(1)} %fusion.15, bf16[2048,5632]{1,0:T(8,128)(2,1)} %all-gather.11.cloned.1.call-done), kind=kOutput, calls=%fused_computation.8 | convolution fusion | flops 2963603456 | bytes 33685504 | tf_op jit(solution)/shard_map/dot_general | solution.py:89
  506.3 0.7 all-gather.19.cloned.1.call-update
  507.5 0.6 slice.92
  508.1 0.7 pad_add_fusion
  509.1 136.8 %all-gather.9.cloned.1.call-done = bf16[2048,6144]{1,0:T(8,128)(2,1)} async-done(((bf16[64,6144]{1,0:T(8,128)(2,1)}), bf16[2048,6144]{1,0:T(8,128)(2,1)}) %all-gather.9.cloned.1.call-update) | async-done | bytes 25165840 | tf_op jit(solution)/shard_map/all_gather | solution.py:83
  645.9 13.5 %convolution_add_fusion = f32[128,6144]{1,0:T(8,128)} fusion(bf16[128,2048]{1,0:T(8,128)(2,1)S(1)} %fusion.15, bf16[2048,6144]{1,0:T(8,128)(2,1)} %all-gather.9.cloned.1.call-done, f32[6144]{0:T(1024)S(1)} %copy-done.15), kind=kOutput, calls=%fused_computation.5 | convolution fusion | flops 3222011904 | bytes 28860416 | tf_op jit(solution)/shard_map/dot_general | solution.py:89
  659.5 3.6 copy.43
  663.0 1.7 slice_bitcast_fusion.1
  664.9 0.6 fusion.35
  665.9 1.2 copy-done.4
  667.1 1.9 multiply_reduce_fusion
  669.0 0.6 multiply_convert_fusion.3
  669.6 0.8 fusion.5
  671.2 0.9 convolution_bitcast_fusion
  672.0 1.9 convert_reduce_fusion
  674.0 2.5 fusion.13
  676.5 1.9 copy.45
  678.4 1.4 pad_maximum_fusion.1
  679.8 3.6 all-to-all-start.2
  683.7 83.4 %all-to-all-done.2 = bf16[128,4,1920]{0,2,1:T(8,128)(2,1)S(1)} async-done(((bf16[128,4,1920]{0,2,1:T(8,128)(2,1)}), bf16[128,4,1920]{0,2,1:T(8,128)(2,1)S(1)}, u32[]{:S(2)}, u32[]{:S(2)}) %all-to-all-start.2) | async-done | bytes 1966112 | tf_op jit(solution)/shard_map/all_to_all | solution.py:176
  767.2 2.4 copy.55
  769.6 9.7 convolution_convert_fusion.3
  779.3 1.4 copy-done.2
  780.7 14.2 %fusion.38 = f32[128,2048]{1,0:T(8,128)} fusion(bf16[128,6144]{0,1:T(8,128)(2,1)S(1)} %bitcast.81, bf16[2048,6144]{1,0:T(8,128)(2,1)} %all-gather.9.cloned.1.call-done), kind=kOutput, calls=%fused_computation.108 | convolution fusion | flops 3221225472 | bytes 27787264 | tf_op jit(solution)/shard_map/dot_general | solution.py:152
  794.8 12.5 convolution_add_fusion.2
  807.3 13.6 %fusion.19 = (f32[2048]{0:T(1024)S(1)}, f32[128]{0:T(128)S(1)}, f32[128]{0:T(128)S(1)}, f32[2048]{0:T(1024)S(1)}, f32[128,2048]{1,0:T(8,128)}) fusion(bf16[128,2048]{1,0:T(8,128)(2,1)S(1)} %copy-done.6, f32[128]{0:T(128)S(1)} %add_rsqrt_fusion, f32[128]{0:T(128)S(1)} %broadcast_multiply_fusion.2, f32[2048]{0:T(1024)S(1)} %copy-done.14, ...), kind=kOutput, calls=%fused_computation.49 | convolution fusion | flops 2955669504 | bytes 27158528 | tf_op jit(solution)/shard_map/dot_general | solution.py:156
  821.7 2.0 reshape.253
  823.7 2.8 maximum_maximum_fusion
  826.5 3.5 all-to-all-start.1
  830.1 0.8 copy.63
  830.9 50.9 %all-to-all-done.1 = f32[128,4,512]{0,2,1:T(8,128)S(1)} async-done(((f32[128,4,512]{0,2,1:T(8,128)}), f32[128,4,512]{0,2,1:T(8,128)S(1)}, u32[]{:S(2)}, u32[]{:S(2)}) %all-to-all-start.1) | async-done | bytes 1048608 | tf_op jit(solution)/shard_map/all_to_all | solution.py:178
  881.8 3.5 all-to-all-start
  885.4 27.3 %all-to-all-done = bf16[128,4,512]{2,0,1:T(8,128)(2,1)S(1)} async-done(((bf16[128,4,512]{2,0,1:T(8,128)(2,1)}), bf16[128,4,512]{2,0,1:T(8,128)(2,1)S(1)}, u32[]{:S(2)}, u32[]{:S(2)}) %all-to-all-start) | async-done | bytes 524320 | tf_op jit(solution)/shard_map/all_to_all | solution.py:175
  912.7 7.7 convolution_convert_fusion
  920.4 40.2 %all-gather.19.cloned.1.call-done = bf16[512,5632]{1,0:T(8,128)(2,1)} async-done(((bf16[128,5632]{1,0:T(8,128)(2,1)}), bf16[512,5632]{1,0:T(8,128)(2,1)}) %all-gather.19.cloned.1.call-update) | async-done | bytes 5767184 | tf_op jit(solution)/shard_map/all_gather | solution.py:182
  960.6 7.6 convolution_convert_fusion.1
  968.3 108.3 %all-gather.17.cloned.1.call-done = bf16[512,6144]{0,1:T(8,128)(2,1)} async-done(((bf16[128,6144]{0,1:T(8,128)(2,1)}), bf16[512,6144]{0,1:T(8,128)(2,1)}) %all-gather.17.cloned.1.call-update) | async-done | bytes 6291472 | tf_op jit(solution)/shard_map/all_gather | solution.py:181
  1076.5 8.4 convolution_convert_fusion.2
  1084.9 10.8 pad_maximum_fusion
  1095.8 1.2 copy-done.9
  1097.1 1.3 fusion.22
  1098.4 16.9 %fusion.2 = bf16[128,2048]{1,0:T(8,128)(2,1)} fusion(bf16[128,7680]{0,1:T(8,128)(2,1)} %bitcast.10, bf16[7680,2048]{1,0:T(8,128)(2,1)} %all-gather.15.cloned.1.call-done, bf16[128,2048]{1,0:T(8,128)(2,1)S(1)} %copy-done.6, f32[128]{0:T(128)S(1)} %compare_convert_fusion), kind=kOutput, calls=%fused_computation.17 | convolution fusion | flops 4027580416 | bytes 34472448 | tf_op jit(solution)/shard_map/dot_general | solution.py:111
  1115.3 32.3 %reduce-scatter.5.cloned.1.call-done = bf16[240,2048]{1,0:T(8,128)(2,1)} async-done(((bf16[1920,2048]{1,0:T(8,128)(2,1)}), bf16[240,2048]{1,0:T(8,128)(2,1)}) %reduce-scatter.5.cloned.1.call-update) | async-done | bytes 983056 | tf_op jit(solution)/shard_map/reduce_scatter | solution.py:199
  1147.6 2.5 slice.137
  1150.0 0.8 slice.134
  1150.9 122.3 %reduce-scatter.3.cloned.1.call-done = bf16[64,17536]{1,0:T(8,128)(2,1)} async-done(((bf16[512,17536]{1,0:T(8,128)(2,1)}), bf16[64,17536]{1,0:T(8,128)(2,1)}) %reduce-scatter.3.cloned.1.call-update) | async-done | bytes 2244624 | tf_op jit(solution)/shard_map/reduce_scatter | solution.py:196
  1273.1 2.1 convert_element_type.111
  1275.2 0.7 slice_reduce_fusion
  1276.0 0.7 reshape.254
  1276.7 1.9 fusion.34
  1278.6 1.2 slice.133
  (83 shorter events, 5.0 us)
Async XLA Ops:
  7.2 4.5 copy-start.17
  7.2 4.7 copy-start.11
  7.2 151.0 %all-gather.13.cloned.1.call-start = ((), (), s32[]{:S(2)}) async-start(), calls=%async_computation.7 | async-start | bytes 23789568 | tf_op jit(solution)/shard_map/all_gather | solution.py:85
  7.9 5.0 copy-start.6
  7.9 336.8 %all-gather.15.cloned.1.call-start = ((), (), s32[]{:S(2)}) async-start(), calls=%async_computation.8 | async-start | bytes 32440320 | tf_op jit(solution)/shard_map/all_gather | solution.py:113
  10.3 3.2 copy-start.14
  10.3 3.2 copy-start.16
  10.3 480.1 %all-gather.11.cloned.1.call-start = ((), (), s32[]{:S(2)}) async-start(), calls=%async_computation.6 | async-start | bytes 23789568 | tf_op jit(solution)/shard_map/all_gather | solution.py:84
  11.0 634.9 %all-gather.9.cloned.1.call-start = ((), (), s32[]{:S(2)}) async-start(), calls=%async_computation.5 | async-start | bytes 25952256 | tf_op jit(solution)/shard_map/all_gather | solution.py:83
  11.6 758.0 %all-gather.23.cloned.1.call-start = ((), (), s32[]{:S(2)}) async-start(), calls=%async_computation.13 | async-start | bytes 2621440 | tf_op jit(solution)/shard_map/all_gather | solution.py:184
  12.9 899.8 %all-gather.21.cloned.1.call-start = ((), (), s32[]{:S(2)}) async-start(), calls=%async_computation.11 | async-start | bytes 7208960 | tf_op jit(solution)/shard_map/all_gather | solution.py:183
  13.9 330.9 %copy-start.8 = (bf16[128,2048]{1,0:T(8,128)(2,1)S(1)}, bf16[128,2048]{1,0:T(8,128)(2,1)}, u32[]{:S(2)}) copy-start(bf16[128,2048]{1,0:T(8,128)(2,1)} %fusion.21) | copy-start | bytes 1572868
  359.1 2.8 copy-start.3
  506.2 139.7 %copy-start.15 = (f32[6144]{0:T(1024)S(1)}, f32[6144]{0:T(1024)}, u32[]{:S(2)}) copy-start(f32[6144]{0:T(1024)} %param.15) | copy-start | bytes 73732
  506.2 454.4 %all-gather.19.cloned.1.call-start = ((), (), s32[]{:S(2)}) async-start(), calls=%async_computation.10 | async-start | bytes 7208960 | tf_op jit(solution)/shard_map/all_gather | solution.py:182
  507.0 569.5 %all-gather.17.cloned.1.call-start = ((), (), s32[]{:S(2)}) async-start(), calls=%async_computation.9 | async-start | bytes 7864320 | tf_op jit(solution)/shard_map/all_gather | solution.py:181
  664.9 2.1 copy-start.4
  676.5 1.9 copy-start.13
  679.8 87.4 %all-to-all-start.2 = ((bf16[128,4,1920]{0,2,1:T(8,128)(2,1)}), bf16[128,4,1920]{0,2,1:T(8,128)(2,1)S(1)}, u32[]{:S(2)}, u32[]{:S(2)}) async-start(bf16[128,4,1920]{0,2,1:T(8,128)(2,1)} %bitcast.28), calls=%async_computation.3 | async-start | bytes 3932160 | tf_op jit(solution)/shard_map/all_to_all | solution.py:176
  683.4 464.1 %reduce-scatter.5.cloned.1.call-start = ((), (), s32[]{:S(2)}) async-start(), calls=%async_computation.14 | async-start | bytes 8847360 | tf_op jit(solution)/shard_map/reduce_scatter | solution.py:199
  779.3 1.4 copy-start.2
  794.8 12.5 copy-start.7
  826.5 55.2 %all-to-all-start.1 = ((f32[128,4,512]{0,2,1:T(8,128)}), f32[128,4,512]{0,2,1:T(8,128)S(1)}, u32[]{:S(2)}, u32[]{:S(2)}) async-start(f32[128,4,512]{0,2,1:T(8,128)} %bitcast.26), calls=%async_computation.1 | async-start | bytes 2097152 | tf_op jit(solution)/shard_map/all_to_all | solution.py:178
  881.8 30.9 %all-to-all-start = ((bf16[128,4,512]{2,0,1:T(8,128)(2,1)}), bf16[128,4,512]{2,0,1:T(8,128)(2,1)S(1)}, u32[]{:S(2)}, u32[]{:S(2)}) async-start(bf16[128,4,512]{2,0,1:T(8,128)(2,1)} %bitcast.79), calls=%async_computation | async-start | bytes 1048576 | tf_op jit(solution)/shard_map/all_to_all | solution.py:175
  885.3 387.9 %reduce-scatter.3.cloned.1.call-start = ((), (), s32[]{:S(2)}) async-start(), calls=%async_computation.12 | async-start | bytes 20201472 | tf_op jit(solution)/shard_map/reduce_scatter | solution.py:196
  1076.5 8.4 copy-start
  1076.5 8.4 copy-start.1
  1095.7 1.2 copy-start.9
  1095.7 1.4 copy-start.12
  1147.6 2.5 copy-start.10
  1273.1 2.8 copy-start.5
Sparse Core Ops, SparseCore 0:
  10.9 147.2 all-gather.12
  161.7 182.9 all-gather.14
  347.6 142.7 all-gather.10
  493.1 152.7 all-gather.8
  647.9 57.1 all-gather.22
  707.2 120.0 all-gather.20
  829.4 131.1 all-gather.18
  962.8 113.6 all-gather.16
  1080.0 67.5 reduce-scatter.4
  1151.6 121.4 reduce-scatter.2
where the time goes:
time: 1300 us; the launch traced here: 1290 us
  waiting for transfers between devices  1050 us (81%)
  matrix products  154 us (12%)
  local copies, waits for them, and re-layouts  32 us (2%)
  other arithmetic  27.1 us (2%)
  between operations  14.9 us (1%)
    all_gather x1, waiting for transfers between devices, on_device(): lax.all_gather(mixer, ('dp', 'fsdp'), axis=0, tiled=True)  174 us
    all_gather x1, waiting for transfers between devices, on_device(): lax.all_gather(w_up, ('dp', 'fsdp'), axis=0, tiled=True)  144 us
    all_gather x1, waiting for transfers between devices, on_device(): lax.all_gather(w_qkv, ('dp', 'fsdp'), axis=0, tiled=True)  137 us
    all_gather x1, waiting for transfers between devices, on_device(): lax.all_gather(w_gate, ('dp', 'fsdp'), axis=0, tiled=True)  125 us
    reduce_scatter x1, waiting for transfers between devices, on_device(): lax.psum_scatter(input_part.astype(jnp.bfloat16), 'fsdp', scatter_dimensi...  122 us
    all_gather x1, waiting for transfers between devices, on_device(): lax.all_gather(grad_proj, 'dp', axis=0, tiled=True)  108 us
    all_to_all x1, waiting for transfers between devices, on_device(): lax.all_to_all(joined, 'dp', split_axis=1, concat_axis=0, tiled=True)  83.4 us
    all_to_all x1, waiting for transfers between devices, on_device(): lax.all_to_all(jnp.transpose(stats), 'dp', split_axis=1, concat_axis=0, t...  50.9 us
  transfers between devices with their start and end apart: 13, of which 11 were waited for; matrix products, arithmetic and copies ran while one was open for 16% of the time, Pallas kernels for 0%

commit v1 on v0

--- a/solution.py
+++ b/solution.py
@@ -10,6 +10,27 @@
 NEG = -1e30
 CONTRACT_ROWS = (((0,), (0,)), ((), ()))
 CONTRACT_COLS = (((1,), (1,)), ((), ()))
+
+
+def gather_around(x, axis, dim):
+    size, here, span = (lax.axis_size(axis), lax.axis_index(axis), x.shape[dim])
+    right = [(i, (i + 1) % size) for i in range(size)]
+    backward = [(i, (i - 1) % size) for i in range(size)]
+    result = jnp.zeros((*x.shape[:dim], size * span, *x.shape[dim + 1 :]), x.dtype)
+    result = lax.dynamic_update_slice_in_dim(result, x, here * span, axis=dim)
+    from_left = from_right = x
+    half = size // 2
+    for step in range(1, half + 1):
+        from_left = lax.ppermute(from_left, axis, right)
+        result = lax.dynamic_update_slice_in_dim(
+            result, from_left, (here - step) % size * span, axis=dim
+        )
+        if step < size - half:
+            from_right = lax.ppermute(from_right, axis, backward)
+            result = lax.dynamic_update_slice_in_dim(
+                result, from_right, (here + step) % size * span, axis=dim
+            )
+    return result
 
 
 def block_terms(lengths_row, rows_tok):
@@ -179,7 +200,7 @@
     stat_sum = jnp.transpose(jnp.sum(stat_parts.reshape(-1, stats.shape[1], group_rows), axis=0))
     pieces = (
         lax.all_gather(grad_proj, "dp", axis=0, tiled=True),
-        lax.all_gather(grad_gate, "dp", axis=0, tiled=True),
+        gather_around(grad_gate, "dp", 0),
         lax.all_gather(grad_up, "dp", axis=0, tiled=True),
         lax.all_gather(masked, "dp", axis=0, tiled=True),
     )

time: 1300 us -> 1280 us (0.985)
  waiting for transfers between devices: 1050 us -> 973 us
  starting transfers between devices: 11.6 us -> 51.4 us
  local copies, waits for them, and re-layouts: 32 us -> 45.2 us
    all_gather x1, waiting for transfers between devices: 108 us -> 31.1 us  [on_device(): lax.all_gather(grad_proj, 'dp', axis=0, tiled=True)]
    all_gather x1 -> x0, waiting for transfers between devices: 40.2 us -> none  [on_device(): lax.all_gather(grad_gate, 'dp', axis=0, tiled=True)]
    ppermute x0 -> x3, waiting for transfers between devices: none -> 37.1 us  [the longest x1 37.1 us: gather_around(): from_right = lax.ppermute(from_right, axis, backward)]
    all_to_all x1, starting transfers between devices: 3.47 us -> 32.7 us  [on_device(): lax.all_to_all(normed, 'dp', split_axis=1, concat_axis=0, tiled=True)]
    all_to_all x1, waiting for transfers between devices: 27.3 us -> 52.9 us  [on_device(): lax.all_to_all(normed, 'dp', split_axis=1, concat_axis=0, tiled=True)]
    all_to_all x1, waiting for transfers between devices: 50.9 us -> 25.6 us  [on_device(): lax.all_to_all(jnp.transpose(stats), 'dp', split_axis=1, concat_axis=0, t...]
  transfers between devices with their start and end apart: 13 -> 15, of which waited for: 11 -> 11; matrix products, arithmetic and copies ran while one was open for 16% -> 17% of each run, Pallas kernels for 0% -> 0%
where the time goes in v1:
time: 1280 us; the launch traced here: 1270 us
  waiting for transfers between devices  973 us (76%)
  matrix products  152 us (12%)
  starting transfers between devices  51.4 us (4%)
  local copies, waits for them, and re-layouts  45.2 us (4%)
  other arithmetic  32.3 us (3%)
  between operations  14.5 us (1%)
    all_gather x1, waiting for transfers between devices, on_device(): lax.all_gather(mixer, ('dp', 'fsdp'), axis=0, tiled=True)  174 us
    all_gather x1, waiting for transfers between devices, on_device(): lax.all_gather(w_up, ('dp', 'fsdp'), axis=0, tiled=True)  144 us
    all_gather x1, waiting for transfers between devices, on_device(): lax.all_gather(w_qkv, ('dp', 'fsdp'), axis=0, tiled=True)  137 us
    all_gather x1, waiting for transfers between devices, on_device(): lax.all_gather(w_gate, ('dp', 'fsdp'), axis=0, tiled=True)  125 us
    reduce_scatter x1, waiting for transfers between devices, on_device(): lax.psum_scatter(input_part.astype(jnp.bfloat16), 'fsdp', scatter_dimensi...  122 us
    all_to_all x1, waiting for transfers between devices, on_device(): lax.all_to_all(joined, 'dp', split_axis=1, concat_axis=0, tiled=True)  87.9 us
    all_to_all x1, waiting for transfers between devices, on_device(): lax.all_to_all(normed, 'dp', split_axis=1, concat_axis=0, tiled=True)  52.9 us
    dot_general x3, matrix products, on_device(): jnp.dot(columns, piece, preferred_element_type=jnp.float32)  41.9 us
  transfers between devices with their start and end apart: 15, of which 11 were waited for; matrix products, arithmetic and copies ran while one was open for 17% of the time, Pallas kernels for 0%

profile of v1, /device:TPU:0, one launch (start us, length us, event | category | flops | bytes accessed | tf_op | source)
XLA Modules:
  0.0 1268.1 jit_solution(1918029391175718902)
XLA Ops:
  8.0 2.3 pad_maximum_fusion.2
  11.9 0.9 fusion.21
  13.9 144.3 %all-gather.12.cloned.1.call-done = bf16[2048,5632]{1,0:T(8,128)(2,1)} async-done(((bf16[64,5632]{1,0:T(8,128)(2,1)}), bf16[2048,5632]{1,0:T(8,128)(2,1)}) %all-gather.12.cloned.1.call-update) | async-done | bytes 23068688 | tf_op jit(solution)/shard_map/all_gather | solution.py:106
  158.2 12.3 fusion.36
  170.5 174.2 %all-gather.14.cloned.1.call-done = bf16[7680,2048]{1,0:T(8,128)(2,1)} async-done(((bf16[240,2048]{1,0:T(8,128)(2,1)}), bf16[7680,2048]{1,0:T(8,128)(2,1)}) %all-gather.14.cloned.1.call-update) | async-done | bytes 31457296 | tf_op jit(solution)/shard_map/all_gather | solution.py:134
  344.7 14.4 %fusion.37 = f32[128,7680]{0,1:T(8,128)S(1)} fusion(bf16[128,2048]{1,0:T(8,128)(2,1)S(1)} %copy-done.10, bf16[7680,2048]{1,0:T(8,128)(2,1)} %all-gather.14.cloned.1.call-done), kind=kOutput, calls=%fused_computation.111 | convolution fusion | flops 4026531840 | bytes 35913728 | tf_op jit(solution)/shard_map/dot_general | solution.py:139
  359.1 1.9 slice.132
  361.1 0.9 copy-done.3
  362.0 3.4 copy.50
  365.4 125.0 %all-gather.10.cloned.1.call-done = bf16[2048,5632]{1,0:T(8,128)(2,1)} async-done(((bf16[64,5632]{1,0:T(8,128)(2,1)}), bf16[2048,5632]{1,0:T(8,128)(2,1)}) %all-gather.10.cloned.1.call-update) | async-done | bytes 23068688 | tf_op jit(solution)/shard_map/all_gather | solution.py:105
  490.4 16.0 %multiply_convert_fusion = (bf16[128,5632]{1,0:T(8,128)(2,1)}, bf16[128,5632]{1,0:T(8,128)(2,1)}, f32[128,5632]{1,0:T(8,128)}) fusion(f32[128,5632]{1,0:T(8,128)} %copy.50, f32[128,5632]{1,0:T(8,128)} %fusion.36, bf16[128,2048]{1,0:T(8,128)(2,1)S(1)} %fusion.15, bf16[2048,5632]{1,0:T(8,128)(2,1)} %all-gather.10.cloned.1.call-done), kind=kOutput, calls=%fused_computation.8 | convolution fusion | flops 2958557184 | bytes 35127296 | tf_op jit(solution)/shard_map/dot_general | solution.py:110
  508.5 137.5 %all-gather.8.cloned.1.call-done = bf16[2048,6144]{1,0:T(8,128)(2,1)} async-done(((bf16[64,6144]{1,0:T(8,128)(2,1)}), bf16[2048,6144]{1,0:T(8,128)(2,1)}) %all-gather.8.cloned.1.call-update) | async-done | bytes 25165840 | tf_op jit(solution)/shard_map/all_gather | solution.py:104
  646.0 13.6 %convolution_add_fusion = f32[128,6144]{1,0:T(8,128)} fusion(bf16[128,2048]{1,0:T(8,128)(2,1)S(1)} %fusion.15, bf16[2048,6144]{1,0:T(8,128)(2,1)} %all-gather.8.cloned.1.call-done, f32[6144]{0:T(1024)S(1)} %copy-done.16), kind=kOutput, calls=%fused_computation.5 | convolution fusion | flops 3222011904 | bytes 28860416 | tf_op jit(solution)/shard_map/dot_general | solution.py:110
  659.6 3.6 copy.43
  663.1 1.7 slice_bitcast_fusion.1
  666.0 1.2 copy-done.4
  667.2 1.9 multiply_reduce_fusion
  669.7 0.8 fusion.5
  671.3 0.9 convolution_bitcast_fusion
  672.1 1.9 convert_reduce_fusion
  674.2 2.5 fusion.13
  676.7 1.9 copy.45
  678.6 1.4 pad_maximum_fusion.1
  680.0 4.4 all-to-all-start.2
  684.5 3.3 broadcast_in_dim.40
  687.8 1.4 copy-done.8
  689.2 4.9 constant_dynamic-update-slice_fusion.3
  694.1 2.1 collective-permute-start
  696.2 14.2 %fusion.38 = f32[128,2048]{1,0:T(8,128)} fusion(bf16[128,6144]{0,1:T(8,128)(2,1)S(1)} %bitcast.81, bf16[2048,6144]{1,0:T(8,128)(2,1)} %all-gather.8.cloned.1.call-done), kind=kOutput, calls=%fused_computation.112 | convolution fusion | flops 3221225472 | bytes 27787264 | tf_op jit(solution)/shard_map/dot_general | solution.py:173
  710.4 87.9 %all-to-all-done.2 = bf16[128,4,1920]{0,2,1:T(8,128)(2,1)} async-done(((bf16[128,4,1920]{0,2,1:T(8,128)(2,1)}), bf16[128,4,1920]{0,2,1:T(8,128)(2,1)}, u32[]{:S(2)}, u32[]{:S(2)}) %all-to-all-start.2) | async-done | bytes 1966112 | tf_op jit(solution)/shard_map/all_to_all | solution.py:197
  798.2 2.8 copy.55
  801.1 7.9 convolution_convert_fusion.3
  809.0 12.5 convolution_add_fusion.2
  821.5 13.5 %fusion.19 = (f32[2048]{0:T(1024)S(1)}, f32[128]{0:T(128)S(1)}, f32[128]{0:T(128)S(1)}, f32[2048]{0:T(1024)S(1)}, f32[128,2048]{1,0:T(8,128)}) fusion(bf16[128,2048]{1,0:T(8,128)(2,1)S(1)} %copy-done.6, f32[128]{0:T(128)S(1)} %add_rsqrt_fusion, f32[128]{0:T(128)S(1)} %broadcast_multiply_fusion.2, f32[2048]{0:T(1024)S(1)} %copy-done.15, ...), kind=kOutput, calls=%fused_computation.49 | convolution fusion | flops 2955669504 | bytes 27158528 | tf_op jit(solution)/shard_map/dot_general | solution.py:177
  835.0 1.0 reshape.253
  836.4 1.4 copy.54
  837.8 2.8 maximum_maximum_fusion
  840.6 3.5 all-to-all-start.1
  844.1 3.8 collective-permute-start.1
  847.9 3.9 collective-permute-start.2
  851.8 0.8 copy.63
  852.6 2.6 constant_dynamic-update-slice_fusion.2
  855.2 25.6 %all-to-all-done.1 = f32[128,4,512]{0,2,1:T(8,128)S(1)} async-done(((f32[128,4,512]{0,2,1:T(8,128)}), f32[128,4,512]{0,2,1:T(8,128)S(1)}, u32[]{:S(2)}, u32[]{:S(2)}) %all-to-all-start.1) | async-done | bytes 1048608 | tf_op jit(solution)/shard_map/all_to_all | solution.py:199
  880.8 32.7 %all-to-all-start = ((bf16[128,4,512]{2,0,1:T(8,128)(2,1)}), bf16[128,4,512]{2,0,1:T(8,128)(2,1)S(1)}, u32[]{:S(2)}, u32[]{:S(2)}) async-start(bf16[128,4,512]{2,0,1:T(8,128)(2,1)} %bitcast.79), calls=%async_computation | async-start | bytes 1048576 | tf_op jit(solution)/shard_map/all_to_all | solution.py:196
  913.7 37.1 %collective-permute-done.1 = bf16[128,5632]{1,0:T(8,128)(2,1)} collective-permute-done((bf16[128,5632]{1,0:T(8,128)(2,1)}, bf16[128,5632]{1,0:T(8,128)(2,1)}, u32[]{:S(2)}, u32[]{:S(2)}) %collective-permute-start.1) | collective-permute-done | bytes 1441824 | tf_op jit(solution)/shard_map/ppermute | solution.py:29
  950.8 2.6 constant_dynamic-update-slice_fusion.1
  953.4 2.6 constant_dynamic-update-slice_fusion
  956.0 52.9 %all-to-all-done = bf16[128,4,512]{2,0,1:T(8,128)(2,1)S(1)} async-done(((bf16[128,4,512]{2,0,1:T(8,128)(2,1)}), bf16[128,4,512]{2,0,1:T(8,128)(2,1)S(1)}, u32[]{:S(2)}, u32[]{:S(2)}) %all-to-all-start) | async-done | bytes 524320 | tf_op jit(solution)/shard_map/all_to_all | solution.py:196
  1008.9 7.6 convolution_convert_fusion.1
  1016.5 7.6 convolution_convert_fusion
  1024.2 31.1 %all-gather.16.cloned.1.call-done = bf16[512,6144]{0,1:T(8,128)(2,1)} async-done(((bf16[128,6144]{0,1:T(8,128)(2,1)}), bf16[512,6144]{0,1:T(8,128)(2,1)}) %all-gather.16.cloned.1.call-update) | async-done | bytes 6291472 | tf_op jit(solution)/shard_map/all_gather | solution.py:202
  1055.2 8.3 convolution_convert_fusion.2
  1063.6 11.2 pad_maximum_fusion
  1074.8 1.2 copy-done.11
  1076.2 1.3 fusion.22
  1077.5 16.9 %fusion.2 = bf16[128,2048]{1,0:T(8,128)(2,1)} fusion(bf16[128,7680]{0,1:T(8,128)(2,1)} %bitcast.10, bf16[7680,2048]{1,0:T(8,128)(2,1)} %all-gather.14.cloned.1.call-done, bf16[128,2048]{1,0:T(8,128)(2,1)S(1)} %copy-done.6, f32[128]{0:T(128)S(1)} %compare_convert_fusion), kind=kOutput, calls=%fused_computation.17 | convolution fusion | flops 4027580416 | bytes 34472448 | tf_op jit(solution)/shard_map/dot_general | solution.py:132
  1094.4 33.8 %reduce-scatter.5.cloned.1.call-done = bf16[240,2048]{1,0:T(8,128)(2,1)} async-done(((bf16[1920,2048]{1,0:T(8,128)(2,1)}), bf16[240,2048]{1,0:T(8,128)(2,1)}) %reduce-scatter.5.cloned.1.call-update) | async-done | bytes 983056 | tf_op jit(solution)/shard_map/reduce_scatter | solution.py:220
  1128.3 1.8 slice.134
  1130.0 2.4 slice.137
  1132.4 121.6 %reduce-scatter.3.cloned.1.call-done = bf16[64,17536]{1,0:T(8,128)(2,1)} async-done(((bf16[512,17536]{1,0:T(8,128)(2,1)}), bf16[64,17536]{1,0:T(8,128)(2,1)}) %reduce-scatter.3.cloned.1.call-update) | async-done | bytes 2244624 | tf_op jit(solution)/shard_map/reduce_scatter | solution.py:217
  1254.0 0.8 slice.140
  1255.5 2.1 convert_element_type.111
  1258.2 1.2 slice.133
  1259.5 1.9 fusion.34
  (93 shorter events, 10.3 us)
Async XLA Ops:
  7.2 4.5 copy-start.18
  7.2 4.7 copy-start.12
  7.2 151.0 %all-gather.12.cloned.1.call-start = ((), (), s32[]{:S(2)}) async-start(), calls=%async_computation.7 | async-start | bytes 23789568 | tf_op jit(solution)/shard_map/all_gather | solution.py:106
  7.9 5.0 copy-start.6
  7.9 336.8 %all-gather.14.cloned.1.call-start = ((), (), s32[]{:S(2)}) async-start(), calls=%async_computation.8 | async-start | bytes 32440320 | tf_op jit(solution)/shard_map/all_gather | solution.py:134
  10.3 3.2 copy-start.15
  10.3 3.2 copy-start.17
  10.3 480.1 %all-gather.10.cloned.1.call-start = ((), (), s32[]{:S(2)}) async-start(), calls=%async_computation.6 | async-start | bytes 23789568 | tf_op jit(solution)/shard_map/all_gather | solution.py:105
  11.0 635.0 %all-gather.8.cloned.1.call-start = ((), (), s32[]{:S(2)}) async-start(), calls=%async_computation.5 | async-start | bytes 25952256 | tf_op jit(solution)/shard_map/all_gather | solution.py:104
  11.6 789.5 %all-gather.20.cloned.1.call-start = ((), (), s32[]{:S(2)}) async-start(), calls=%async_computation.12 | async-start | bytes 2621440 | tf_op jit(solution)/shard_map/all_gather | solution.py:205
  12.9 1003.6 %all-gather.18.cloned.1.call-start = ((), (), s32[]{:S(2)}) async-start(), calls=%async_computation.10 | async-start | bytes 7208960 | tf_op jit(solution)/shard_map/all_gather | solution.py:204
  13.9 330.9 %copy-start.10 = (bf16[128,2048]{1,0:T(8,128)(2,1)S(1)}, bf16[128,2048]{1,0:T(8,128)(2,1)}, u32[]{:S(2)}) copy-start(bf16[128,2048]{1,0:T(8,128)(2,1)} %fusion.21) | copy-start | bytes 1572868
  359.1 2.8 copy-start.3
  365.4 280.6 %copy-start.16 = (f32[6144]{0:T(1024)S(1)}, f32[6144]{0:T(1024)}, u32[]{:S(2)}) copy-start(f32[6144]{0:T(1024)} %param.15) | copy-start | bytes 73732
  506.4 548.9 %all-gather.16.cloned.1.call-start = ((), (), s32[]{:S(2)}) async-start(), calls=%async_computation.9 | async-start | bytes 7864320 | tf_op jit(solution)/shard_map/all_gather | solution.py:202
  665.0 2.1 copy-start.4
  676.7 1.9 copy-start.14
  680.0 118.3 %all-to-all-start.2 = ((bf16[128,4,1920]{0,2,1:T(8,128)(2,1)}), bf16[128,4,1920]{0,2,1:T(8,128)(2,1)}, u32[]{:S(2)}, u32[]{:S(2)}) async-start(bf16[128,4,1920]{0,2,1:T(8,128)(2,1)} %bitcast.28), calls=%async_computation.3 | async-start | bytes 3932160 | tf_op jit(solution)/shard_map/all_to_all | solution.py:197
  684.4 443.9 %reduce-scatter.5.cloned.1.call-start = ((), (), s32[]{:S(2)}) async-start(), calls=%async_computation.13 | async-start | bytes 8847360 | tf_op jit(solution)/shard_map/reduce_scatter | solution.py:220
  684.4 3.3 copy-start.7
  684.5 4.8 copy-start.8
  689.2 7.0 copy-start.2
  694.1 153.8 %collective-permute-start = (bf16[128,5632]{1,0:T(8,128)(2,1)}, bf16[128,5632]{1,0:T(8,128)(2,1)}, u32[]{:S(2)}, u32[]{:S(2)}) collective-permute-start(bf16[128,5632]{1,0:T(8,128)(2,1)} %get-tuple-element.17), channel_id=1, source_target_pairs={{0,8},{8,16},{16,24},{24,0},{1,9},{9,17},{17,25},{25,1},{2,10},{10... | collective-permute-start | bytes 4325384 | tf_op jit(solution)/shard_map/ppermute | solution.py:24
  809.0 12.5 copy-start.9
  840.6 40.2 %all-to-all-start.1 = ((f32[128,4,512]{0,2,1:T(8,128)}), f32[128,4,512]{0,2,1:T(8,128)S(1)}, u32[]{:S(2)}, u32[]{:S(2)}) async-start(f32[128,4,512]{0,2,1:T(8,128)} %bitcast.26), calls=%async_computation.1 | async-start | bytes 2097152 | tf_op jit(solution)/shard_map/all_to_all | solution.py:199
  844.1 106.7 %collective-permute-start.1 = (bf16[128,5632]{1,0:T(8,128)(2,1)}, bf16[128,5632]{1,0:T(8,128)(2,1)}, u32[]{:S(2)}, u32[]{:S(2)}) collective-permute-start(bf16[128,5632]{1,0:T(8,128)(2,1)} %get-tuple-element.17), channel_id=1, source_target_pairs={{0,24},{8,0},{16,8},{24,16},{1,25},{9,1},{17,9},{25,17},{2,26},{10... | collective-permute-start | bytes 4325384 | tf_op jit(solution)/shard_map/ppermute | solution.py:29
  847.9 105.5 %collective-permute-start.2 = (bf16[128,5632]{1,0:T(8,128)(2,1)}, bf16[128,5632]{1,0:T(8,128)(2,1)}, u32[]{:S(2)}, u32[]{:S(2)}) collective-permute-start(bf16[128,5632]{1,0:T(8,128)(2,1)} %collective-permute-done), channel_id=1, source_target_pairs={{0,8},{8,16},{16,24},{24,0},{1,9},{9,17},{17,25},{25,1},{2,10},{10... | collective-permute-start | bytes 4325384 | tf_op jit(solution)/shard_map/ppermute | solution.py:24
  880.8 128.1 %all-to-all-start = ((bf16[128,4,512]{2,0,1:T(8,128)(2,1)}), bf16[128,4,512]{2,0,1:T(8,128)(2,1)S(1)}, u32[]{:S(2)}, u32[]{:S(2)}) async-start(bf16[128,4,512]{2,0,1:T(8,128)(2,1)} %bitcast.79), calls=%async_computation | async-start | bytes 1048576 | tf_op jit(solution)/shard_map/all_to_all | solution.py:196
  913.5 340.5 %reduce-scatter.3.cloned.1.call-start = ((), (), s32[]{:S(2)}) async-start(), calls=%async_computation.11 | async-start | bytes 20201472 | tf_op jit(solution)/shard_map/reduce_scatter | solution.py:217
  1055.2 8.3 copy-start
  1055.2 8.3 copy-start.1
  1074.8 1.3 copy-start.11
  1074.8 1.4 copy-start.13
  1255.5 2.8 copy-start.5
Sparse Core Ops, SparseCore 0:
  10.9 147.2 all-gather.11
  161.7 182.9 all-gather.13
  347.6 142.7 all-gather.9
  493.1 152.8 all-gather.7
  648.0 56.6 all-gather.19
  706.7 175.2 all-gather.17
  884.1 171.0 all-gather.15
  1058.7 69.5 reduce-scatter.4
  1132.4 121.4 reduce-scatter.2
